TPU v7x, 32 devices: a whole 2x2x4 slice. The times are simulated.
32 devices in a mesh: dp: 4 (over y, x), tensor: 8 (over z, core).
Axes of the slice: x: 2, y: 2, z: 4, core: 2. Of those that a mesh axis runs over, the one named last changes fastest.
Arguments:
- tokens: bfloat16 [96, 8192], P(('dp', 'tensor')), may hold values from -6 to 6
- weight_store: bfloat16 [2, 192, 128, 128], P(None, 'tensor', 'dp'), may hold values from -0.25 to 0.25
- block_cols: int32 [24, 8], P('tensor'), may hold values from 0 to 63, as said below
- block_count: int32 [24], P('tensor'), may hold values from 1 to 8, 108 in all
- block_home: int32 [8, 24], P('tensor'), may hold values from 0 to 23, each once within a row
- grad_hidden: bfloat16 [96, 3072], P('dp', 'tensor'), may hold values from -6 to 6
Outputs:
- hidden: bfloat16 [96, 3072], P('dp', 'tensor')
- grad_tokens: bfloat16 [96, 8192], P(('dp', 'tensor'))
- grad_weights: bfloat16 [2, 192, 128, 128], P(None, 'tensor', 'dp')
Inputs may be any that keep to these rules, and one draw needn't show every extreme that they name: `block_cols`: the 8 column blocks listed for one hidden block are all different. `block_count`: some hidden block has all 8 slots present. `block_home`: each row is a permutation of 0 to 23.
All inputs are finite; a program needn't handle non-finite values.
Results may differ from a plain program's by a relative error of at most 0.009.
Values may be sent and summed in bfloat16 or wider, within the bound.
A program may use at most 64 MiB of HBM per device.

v0:
```python
import jax
import jax.numpy as jnp
from jax import lax
from jax.sharding import PartitionSpec as P


def body(tokens, weight_store, block_cols, block_count, block_home, grad_hidden):
    rows_here = tokens.shape[0]
    model_width = tokens.shape[1]
    block_size = weight_store.shape[3]
    hidden_blocks, slot_count = block_cols.shape
    all_slots = hidden_blocks * slot_count
    col_blocks = model_width // block_size
    flat_cols = block_cols.reshape(-1)

    def select_blocks(rows):
        shaped = rows.reshape(rows.shape[0], col_blocks, block_size)
        return jnp.take(shaped, flat_cols, axis=1).reshape(
            rows.shape[0], hidden_blocks, slot_count, block_size
        )

    gathered = lax.all_gather(tokens, "tensor", axis=0, tiled=True)
    group_rows = gathered.shape[0]
    blocks = lax.all_gather(weight_store, "dp", axis=2, tiled=True)
    ordered = jnp.take(blocks, block_home[0], axis=1)
    present = (lax.iota(jnp.int32, slot_count)[None, :] < block_count[:, None]).astype(jnp.bfloat16)
    weights = (
        ordered.reshape(2, hidden_blocks, slot_count, block_size, block_size)
        * present[None, :, :, None, None]
    )
    picked = select_blocks(gathered)
    gate_pre = jnp.einsum("thkb,hkbc->thc", picked, weights[0], preferred_element_type=jnp.float32)
    up_pre = jnp.einsum("thkb,hkbc->thc", picked, weights[1], preferred_element_type=jnp.float32)
    gate_sigma = jax.nn.sigmoid(gate_pre)
    activated = gate_pre * gate_sigma
    hidden = (
        (activated * up_pre).astype(jnp.bfloat16).reshape(group_rows, hidden_blocks * block_size)
    )
    grad_in = grad_hidden.reshape(group_rows, hidden_blocks, block_size).astype(jnp.float32)
    grad_gate = (grad_in * up_pre * gate_sigma * (1.0 + gate_pre * (1.0 - gate_sigma))).astype(
        jnp.bfloat16
    )
    grad_up = (grad_in * activated).astype(jnp.bfloat16)
    back_term = jnp.einsum(
        "thc,hkbc->thkb", grad_gate, weights[0], preferred_element_type=jnp.float32
    )
    back_term = back_term + jnp.einsum(
        "thc,hkbc->thkb", grad_up, weights[1], preferred_element_type=jnp.float32
    )
    spread = jnp.zeros((rows_here * lax.axis_size("tensor"), col_blocks, block_size), jnp.float32)
    spread = spread.at[:, flat_cols].add(
        back_term.reshape(rows_here * lax.axis_size("tensor"), all_slots, block_size)
    )
    grad_tokens = lax.psum_scatter(
        spread.reshape(rows_here * lax.axis_size("tensor"), model_width),
        "tensor",
        scatter_dimension=0,
        tiled=True,
    ).astype(jnp.bfloat16)
    fetched = lax.all_gather(tokens, "tensor", axis=0, tiled=True)
    source = select_blocks(fetched)
    part_gate = jnp.einsum("thkb,thc->hkbc", source, grad_gate, preferred_element_type=jnp.float32)
    part_up = jnp.einsum("thkb,thc->hkbc", source, grad_up, preferred_element_type=jnp.float32)
    partial_value = (
        jnp.stack([part_gate, part_up]) * present.astype(jnp.float32)[None, :, :, None, None]
    )
    partial_value = partial_value.reshape(2, all_slots, block_size, block_size)
    grad_store = jnp.zeros_like(partial_value).at[:, block_home[0]].set(partial_value)
    summed = lax.psum_scatter(
        grad_store.astype(jnp.bfloat16), "dp", scatter_dimension=2, tiled=True
    )
    return (hidden, grad_tokens, summed)


def solution(mesh):
    return jax.shard_map(
        body,
        mesh=mesh,
        in_specs=(
            P(("dp", "tensor"), None),
            P(None, "tensor", "dp", None),
            P("tensor", None),
            P("tensor"),
            P("tensor", None),
            P("dp", "tensor"),
        ),
        out_specs=(P("dp", "tensor"), P(("dp", "tensor"), None), P(None, "tensor", "dp", None)),
        check_vma=False,
    )
```

profile of v0, /device:TPU:0, one launch (start us, length us, event | category | flops | bytes accessed | tf_op | source)
XLA Modules:
  0.0 103.6 jit_solution(13636348723635361189)
XLA Ops:
  7.2 0.0 copy-start.2
  7.2 0.0 copy-start.1
  7.2 0.0 all-gather.3.cloned.1.call-start
  7.2 0.7 all-gather.3.cloned.1.call-update
  7.9 0.0 reduce-scatter.2.cloned.1.call-start
  8.0 0.8 reshape.154
  8.7 0.8 reshape.157
  9.5 0.5 broadcast.141
  10.0 1.3 %reduce.3 = s32[24]{0:T(128)S(1)} reduce(s32[1,24]{1,0:T(1,128)} %param.12, s32[]{:T(128)} %broadcast.141), dimensions={0}, to_apply=%param.12.reduce_sub_computation.3 | reduce | bytes 196 | tf_op args[4]
  11.3 0.1 squeeze.14
  11.4 0.7 fusion.15
  12.1 0.1 reshape.162
  12.2 16.8 %all-gather = bf16[8,3,8192]{2,1,0:T(4,128)(2,1)S(1)} all-gather(bf16[1,3,8192]{2,1,0:T(4,128)(2,1)} %bitcast.101), channel_id=1, replica_groups=mesh['dp'=4,'tensor'=8] {'tensor'}, dimensions={0}, use_global_device_ids=true | all-gather | bytes 442368 | tf_op jit(solution)/shard_map/all_gather | solution.py:22
  29.0 0.5 reshape.153
  29.5 0.3 copy.22
  29.8 0.0 copy-done.2
  29.8 0.6 dynamic-slice
  31.1 0.6 gather_fusion.1
  31.7 0.0 copy-done.1
  31.7 0.1 broadcast_select_fusion
  31.8 11.6 %all-gather.3.cloned.1.call-done = bf16[2,24,128,128]{3,2,1,0:T(8,128)(2,1)} async-done(((bf16[2,24,32,128]{3,2,1,0:T(8,128)(2,1)}), bf16[2,24,128,128]{3,2,1,0:T(8,128)(2,1)}) %all-gather.3.cloned.1.call-update) | async-done | bytes 1572880 | tf_op jit(solution)/shard_map/all_gather | solution.py:24
  43.4 2.3 %gather_fusion = bf16[24,2,128,128]{3,2,1,0:T(8,128)(2,1)S(1)} fusion(bf16[2,24,128,128]{3,2,1,0:T(8,128)(2,1)} %all-gather.3.cloned.1.call-done, s32[1024]{0:T(1024)S(1)} %pad_clamp_fusion.1), kind=kCustom, calls=%fused_computation.1 | custom fusion | bytes 3145824 | tf_op jit(solution)/shard_map/jit(_take)/gather | solution.py:25
  45.7 0.1 copy.21
  45.8 0.0 copy-start
  45.8 0.3 select_multiply_fusion
  46.1 0.2 convolution_bitcast_fusion
  46.3 0.2 copy-done
  46.5 0.2 fusion.8
  46.8 0.5 fusion.1
  47.3 0.4 fusion.9
  47.7 0.6 copy.42
  48.3 0.4 fusion.16
  48.8 0.5 convolution_add_fusion
  49.3 2.0 %fusion = f32[24,2,128,128]{3,2,1,0:T(8,128)} fusion(f32[1,24,128,128]{3,2,0,1:T(8,128)S(1)} %bitcast.95, f32[1,24,128,128]{3,2,0,1:T(8,128)S(1)} %bitcast.94, f32[24]{0:T(128)S(1)} %reshape.162), kind=kLoop, calls=%fused_computation.5 | loop fusion | flops 1572864 | bytes 6291552 | tf_op jit(solution)/shard_map/mul | solution.py:65
  51.3 0.4 broadcast_in_dim.34
  51.7 4.7 %scatter_fusion.1 = f32[2,24,128,128]{3,2,1,0:T(8,128)S(1)} fusion(f32[2,24,128,128]{3,2,1,0:T(8,128)S(1)} %broadcast_in_dim.34, s32[24]{0:T(128)S(1)} %fusion.13, f32[24,2,128,128]{3,2,1,0:T(8,128)} %fusion), kind=kCustom, calls=%fused_computation.3 | custom fusion | bytes 9437280 | tf_op jit(solution)/shard_map/scatter | solution.py:68
  56.3 1.4 %convert_element_type.54 = bf16[2,24,128,128]{3,2,1,0:T(8,128)(2,1)} convert(f32[2,24,128,128]{3,2,1,0:T(8,128)S(1)} %scatter_fusion.1) | non-fusion elementwise | flops 786432 | bytes 4718592 | tf_op jit(solution)/shard_map/convert_element_type | solution.py:70
  57.8 0.0 reduce-scatter.2.cloned.1.call-update
  57.8 0.1 broadcast_in_dim.33
  57.8 1.9 %scatter_fusion = f32[24,64,128]{2,0,1:T(8,128)S(1)} fusion(f32[24,64,128]{2,0,1:T(8,128)S(1)} %broadcast_in_dim.33, s32[24]{0:T(128)S(1)} %fusion.14, f32[24,24,128]{2,1,0:T(8,128)S(1)} %bitcast.100), kind=kCustom, calls=%fused_computation.2 | custom fusion | flops 73728 | bytes 884832 | tf_op jit(solution)/shard_map/scatter-add | solution.py:51
  59.8 0.1 copy_bitcast_fusion
  59.8 36.2 %all-reduce.2 = bf16[24,8192]{1,0:T(8,128)(2,1)S(1)} all-reduce(f32[24,8192]{1,0:T(8,128)S(1)} %copy_bitcast_fusion), channel_id=2, replica_groups=mesh['dp'=4,'tensor'=8] {'tensor'}, use_global_device_ids=true, to_apply=%region_1.3.clone | all-reduce | flops 196608 | bytes 1179648
  96.0 0.7 dynamic-slice_convert_fusion
  96.7 0.0 reduce-scatter.2.cloned.1.call-done
  (6 shorter events, 0.0 us)
Async XLA Ops:
  7.2 22.7 %copy-start.2 = (u32[32]{0:T(128)S(1)}, u32[32]{0:T(128)}, u32[]{:S(2)}) copy-start(u32[32]{0:T(128)} %constant.41) | copy-start | bytes 388
  7.2 24.5 %copy-start.1 = (s32[1,24]{1,0:T(1,128)S(1)}, s32[1,24]{1,0:T(1,128)}, u32[]{:S(2)}) copy-start(s32[1,24]{1,0:T(1,128)} %param.12) | copy-start | bytes 292
  7.2 36.2 %all-gather.3.cloned.1.call-start = ((), (), s32[]{:S(2)}) async-start(), calls=%async_computation.1 | async-start | bytes 1966080 | tf_op jit(solution)/shard_map/all_gather | solution.py:24
  7.9 88.8 %reduce-scatter.2.cloned.1.call-start = ((), (), s32[]{:S(2)}) async-start(), calls=%async_computation.2 | async-start | bytes 1966080 | tf_op jit(solution)/shard_map/reduce_scatter | solution.py:69
  45.8 0.7 copy-start
Sparse Core Ops, SparseCore 0:
  9.8 33.5 all-gather.2
  57.9 30.9 reduce-scatter.1
where the time goes:
time: 104 us
  blocking collectives  53 us (51%)
  between operations  14.9 us (14%)
  local copies, waits for them, and re-layouts  13.2 us (13%)
  waiting for transfers between devices  12.3 us (12%)
  other arithmetic  7.79 us (7%)
  matrix products  2.36 us (2%)
    unnamed x1, blocking collectives  36.2 us
    all_gather x1, blocking collectives, body(): gathered = lax.all_gather(tokens, 'tensor', axis=0, tiled=True)  16.8 us
    all_gather x1, waiting for transfers between devices, body(): blocks = lax.all_gather(weight_store, 'dp', axis=2, tiled=True)  11.6 us
    scatter x1, local copies, waits for them, and re-layouts, body(): jnp.zeros_like(partial_value).at[:, block_home[0]].set(partial_value)  4.69 us
    gather x2, local copies, waits for them, and re-layouts, body(): ordered = jnp.take(blocks, block_home[0], axis=1)  2.36 us
  transfers between devices with their start and end apart: 2, of which 1 were waited for; matrix products, arithmetic and copies ran while one was open for 9% of the time, Pallas kernels for 0%

commit v1 on v0

--- a/solution.py
+++ b/solution.py
@@ -19,7 +19,18 @@
             rows.shape[0], hidden_blocks, slot_count, block_size
         )
 
-    gathered = lax.all_gather(tokens, "tensor", axis=0, tiled=True)
+    formed = lax.axis_size("tensor")
+    aux = lax.axis_index("tensor")
+    ready, z_new, local_next = (formed, aux, tokens.shape[0])
+    newest, opened = (tokens, 1)
+    while opened < ready:
+        store = []
+        for t in range(ready):
+            store.append((t, (t - opened) % ready))
+        far_arr = lax.ppermute(newest, "tensor", store)
+        newest = jnp.concatenate([newest, far_arr], axis=0)
+        opened = 2 * opened
+    gathered = jnp.roll(newest, z_new * local_next, axis=0)
     group_rows = gathered.shape[0]
     blocks = lax.all_gather(weight_store, "dp", axis=2, tiled=True)
     ordered = jnp.take(blocks, block_home[0], axis=1)

time: 104 us -> 118 us (1.13)
  waiting for transfers between devices: 12.3 us -> 19.2 us
  starting transfers between devices: 0.08 us -> 6.36 us
  blocking collectives: 53 us -> 49.7 us
  local copies, waits for them, and re-layouts: 13.2 us -> 16.1 us
    ppermute x0 -> x3, waiting for transfers between devices: none -> 18.5 us  [body(): far_arr = lax.ppermute(newest, 'tensor', store)]
    all_gather x1, waiting for transfers between devices: 11.6 us -> 0.02 us  [body(): blocks = lax.all_gather(weight_store, 'dp', axis=2, tiled=True)]
    ppermute x0 -> x3, starting transfers between devices: none -> 6.28 us  [body(): far_arr = lax.ppermute(newest, 'tensor', store)]
    concatenate x0 -> x1, local copies, waits for them, and re-layouts: none -> 2.19 us  [body(): gathered = jnp.roll(newest, z_new * local_next, axis=0)]
    all_gather x1, blocking collectives: 16.8 us -> 15.1 us  [body(): fetched = lax.all_gather(tokens, 'tensor', axis=0, tiled=True)]
    unnamed x1, blocking collectives: 36.2 us -> 34.6 us
  transfers between devices with their start and end apart: 2 -> 5, of which waited for: 1 -> 2; matrix products, arithmetic and copies ran while one was open for 9% -> 11% of each run, Pallas kernels for 0% -> 0%
where the time goes in v1:
time: 118 us; the launch traced here: 117 us
  blocking collectives  49.7 us (42%)
  waiting for transfers between devices  19.2 us (16%)
  local copies, waits for them, and re-layouts  16.1 us (14%)
  between operations  14.9 us (13%)
  other arithmetic  8.67 us (7%)
  starting transfers between devices  6.36 us (5%)
  matrix products  2.36 us (2%)
    unnamed x1, blocking collectives  34.6 us
    ppermute x3, waiting for transfers between devices, body(): far_arr = lax.ppermute(newest, 'tensor', store)  18.5 us
    all_gather x1, blocking collectives, body(): fetched = lax.all_gather(tokens, 'tensor', axis=0, tiled=True)  15.1 us
    ppermute x3, starting transfers between devices, body(): far_arr = lax.ppermute(newest, 'tensor', store)  6.28 us
    scatter x1, local copies, waits for them, and re-layouts, body(): jnp.zeros_like(partial_value).at[:, block_home[0]].set(partial_value)  4.69 us
    gather x2, local copies, waits for them, and re-layouts, body(): ordered = jnp.take(blocks, block_home[0], axis=1)  2.36 us
  transfers between devices with their start and end apart: 5, of which 2 were waited for; matrix products, arithmetic and copies ran while one was open for 11% of the time, Pallas kernels for 0%

profile of v1, /device:TPU:0, one launch (start us, length us, event | category | flops | bytes accessed | tf_op | source)
XLA Modules:
  0.0 117.3 jit_solution(4478348819914803387)
XLA Ops:
  7.2 0.0 copy-start.2
  7.2 0.0 copy-start
  7.2 0.0 all-gather.3.cloned.1.call-start
  7.2 0.7 all-gather.3.cloned.1.call-update
  7.9 0.0 reduce-scatter.2.cloned.1.call-start
  8.0 4.5 %collective-permute-start = (bf16[3,8192]{1,0:T(4,128)(2,1)}, bf16[3,8192]{1,0:T(4,128)(2,1)S(1)}, u32[]{:S(2)}, u32[]{:S(2)}) collective-permute-start(bf16[3,8192]{1,0:T(4,128)(2,1)} %param.8), channel_id=1, source_target_pairs={{0,7},{1,0},{2,1},{3,2},{4,3},{5,4},{6,5},{7,6},{8,15},{9,8},{10,9... | collective-permute-start | bytes 147464 | tf_op jit(solution)/shard_map/ppermute | solution.py:30
  12.5 0.8 reshape.158
  13.3 0.7 fusion.13
  13.9 0.5 broadcast.156
  14.5 1.3 %reduce.3 = s32[24]{0:T(128)S(1)} reduce(s32[1,24]{1,0:T(1,128)} %param.12, s32[]{:T(128)} %broadcast.156), dimensions={0}, to_apply=%param.12.reduce_sub_computation.3 | reduce | bytes 196 | tf_op args[4]
  15.8 0.1 squeeze.14
  15.9 15.1 %all-gather = bf16[8,3,8192]{2,1,0:T(4,128)(2,1)S(1)} all-gather(bf16[1,3,8192]{2,1,0:T(4,128)(2,1)} %bitcast.104), channel_id=1, replica_groups=mesh['dp'=4,'tensor'=8] {'tensor'}, dimensions={0}, use_global_device_ids=true | all-gather | bytes 442368 | tf_op jit(solution)/shard_map/all_gather | solution.py:71
  30.9 0.7 fusion.15
  31.7 0.8 reshape.161
  32.4 0.1 reshape.168
  32.5 0.5 reshape.164
  33.0 0.3 copy.36
  33.3 0.0 copy-done.2
  33.3 0.6 dynamic-slice
  34.6 0.6 gather_fusion.2
  35.2 0.0 collective-permute-done
  35.2 0.0 copy-done
  35.2 0.1 pad_maximum_fusion.1
  35.3 1.0 collective-permute-start.1
  36.3 4.8 %collective-permute-done.1 = bf16[6,8192]{1,0:T(8,128)(2,1)S(1)} collective-permute-done((bf16[6,8192]{1,0:T(8,128)(2,1)S(1)}, bf16[6,8192]{1,0:T(8,128)(2,1)S(1)}, u32[]{:S(2)}, u32[]{:S(2)}) %collective-permute-start.1) | collective-permute-done | bytes 98336 | tf_op jit(solution)/shard_map/ppermute | solution.py:30
  41.1 0.2 pad_maximum_fusion
  41.2 0.7 collective-permute-start.2
  41.9 13.7 %collective-permute-done.2 = bf16[12,8192]{1,0:T(8,128)(2,1)S(1)} collective-permute-done((bf16[12,8192]{1,0:T(8,128)(2,1)S(1)}, bf16[12,8192]{1,0:T(8,128)(2,1)S(1)}, u32[]{:S(2)}, u32[]{:S(2)}) %collective-permute-start.2) | collective-permute-done | bytes 196640 | tf_op jit(solution)/shard_map/ppermute | solution.py:30
  55.7 2.2 %concatenate.17 = bf16[48,8192]{1,0:T(8,128)(2,1)S(1)} concatenate(bf16[3,8192]{1,0:T(4,128)(2,1)S(1)} %copy-done, bf16[3,8192]{1,0:T(4,128)(2,1)S(1)} %collective-permute-done, bf16[6,8192]{1,0:T(8,128)(2,1)S(1)} %collective-permute-done.1, bf16[12,8192]{1,0:T(8,128)(2,1)S(1)} %collective-permute-done.2, bf16[3,8192]{1,0:T(4,128)(2,1)S(1)} %copy-done, ...), dimensions={0} | concatenate | bytes 1572864 | tf_op jit(solution)/shard_map/jit(_roll_dynamic)/concatenate | solution.py:33
  57.9 0.1 copy_bitcast_fusion.1
  58.0 0.6 gather_fusion.1
  58.6 0.1 broadcast_select_fusion
  58.7 0.0 all-gather.3.cloned.1.call-done
  58.7 2.3 %gather_fusion = bf16[24,2,128,128]{3,2,1,0:T(8,128)(2,1)S(1)} fusion(bf16[2,24,128,128]{3,2,1,0:T(8,128)(2,1)} %all-gather.3.cloned.1.call-done, s32[1024]{0:T(1024)S(1)} %pad_clamp_fusion.1), kind=kCustom, calls=%fused_computation.2 | custom fusion | bytes 3145824 | tf_op jit(solution)/shard_map/jit(_take)/gather | solution.py:36
  61.0 0.1 copy.30
  61.1 0.0 copy-start.1
  61.1 0.3 select_multiply_fusion
  61.4 0.2 convolution_bitcast_fusion
  61.6 0.2 copy-done.1
  61.8 0.2 fusion.8
  62.1 0.6 copy.54
  62.7 0.5 fusion.1
  63.2 0.4 fusion.9
  63.7 0.4 fusion.16
  64.1 0.5 convolution_add_fusion
  64.6 2.0 %fusion = f32[24,2,128,128]{3,2,1,0:T(8,128)} fusion(f32[1,24,128,128]{3,2,0,1:T(8,128)S(1)} %bitcast.103, f32[1,24,128,128]{3,2,0,1:T(8,128)S(1)} %bitcast.102, f32[24]{0:T(128)S(1)} %reshape.168), kind=kLoop, calls=%fused_computation.6 | loop fusion | flops 1572864 | bytes 6291552 | tf_op jit(solution)/shard_map/mul | solution.py:76
  66.6 0.4 broadcast_in_dim.34
  67.0 4.7 %scatter_fusion.1 = f32[2,24,128,128]{3,2,1,0:T(8,128)S(1)} fusion(f32[2,24,128,128]{3,2,1,0:T(8,128)S(1)} %broadcast_in_dim.34, s32[24]{0:T(128)S(1)} %fusion.13, f32[24,2,128,128]{3,2,1,0:T(8,128)} %fusion), kind=kCustom, calls=%fused_computation.4 | custom fusion | bytes 9437280 | tf_op jit(solution)/shard_map/scatter | solution.py:79
  71.7 1.4 %convert_element_type.54 = bf16[2,24,128,128]{3,2,1,0:T(8,128)(2,1)} convert(f32[2,24,128,128]{3,2,1,0:T(8,128)S(1)} %scatter_fusion.1) | non-fusion elementwise | flops 786432 | bytes 4718592 | tf_op jit(solution)/shard_map/convert_element_type | solution.py:81
  73.1 0.0 reduce-scatter.2.cloned.1.call-update
  73.1 0.1 broadcast_in_dim.33
  73.2 1.9 %scatter_fusion = f32[24,64,128]{2,0,1:T(8,128)S(1)} fusion(f32[24,64,128]{2,0,1:T(8,128)S(1)} %broadcast_in_dim.33, s32[24]{0:T(128)S(1)} %fusion.14, f32[24,24,128]{2,1,0:T(8,128)S(1)} %bitcast.107), kind=kCustom, calls=%fused_computation.3 | custom fusion | flops 73728 | bytes 884832 | tf_op jit(solution)/shard_map/scatter-add | solution.py:62
  75.1 0.1 copy_bitcast_fusion
  75.2 34.6 %all-reduce.2 = bf16[24,8192]{1,0:T(8,128)(2,1)S(1)} all-reduce(f32[24,8192]{1,0:T(8,128)S(1)} %copy_bitcast_fusion), channel_id=2, replica_groups=mesh['dp'=4,'tensor'=8] {'tensor'}, use_global_device_ids=true, to_apply=%region_1.3.clone | all-reduce | flops 196608 | bytes 1179648
  109.8 0.7 dynamic-slice_convert_fusion
  110.5 0.0 reduce-scatter.2.cloned.1.call-done
  (5 shorter events, 0.0 us)
Async XLA Ops:
  7.2 26.2 %copy-start.2 = (u32[32]{0:T(128)S(1)}, u32[32]{0:T(128)}, u32[]{:S(2)}) copy-start(u32[32]{0:T(128)} %constant.64) | copy-start | bytes 388
  7.2 28.0 %copy-start = (bf16[3,8192]{1,0:T(4,128)(2,1)S(1)}, bf16[3,8192]{1,0:T(4,128)(2,1)}, u32[]{:S(2)}) copy-start(bf16[3,8192]{1,0:T(4,128)(2,1)} %param.8) | copy-start | bytes 147460
  7.2 51.5 %all-gather.3.cloned.1.call-start = ((), (), s32[]{:S(2)}) async-start(), calls=%async_computation.1 | async-start | bytes 1966080 | tf_op jit(solution)/shard_map/all_gather | solution.py:35
  7.9 102.5 %reduce-scatter.2.cloned.1.call-start = ((), (), s32[]{:S(2)}) async-start(), calls=%async_computation.2 | async-start | bytes 1966080 | tf_op jit(solution)/shard_map/reduce_scatter | solution.py:80
  8.0 27.2 %collective-permute-start = (bf16[3,8192]{1,0:T(4,128)(2,1)}, bf16[3,8192]{1,0:T(4,128)(2,1)S(1)}, u32[]{:S(2)}, u32[]{:S(2)}) collective-permute-start(bf16[3,8192]{1,0:T(4,128)(2,1)} %param.8), channel_id=1, source_target_pairs={{0,7},{1,0},{2,1},{3,2},{4,3},{5,4},{6,5},{7,6},{8,15},{9,8},{10,9... | collective-permute-start | bytes 147464 | tf_op jit(solution)/shard_map/ppermute | solution.py:30
  35.3 5.8 %collective-permute-start.1 = (bf16[6,8192]{1,0:T(8,128)(2,1)S(1)}, bf16[6,8192]{1,0:T(8,128)(2,1)S(1)}, u32[]{:S(2)}, u32[]{:S(2)}) collective-permute-start(bf16[6,8192]{1,0:T(8,128)(2,1)S(1)} %pad_maximum_fusion.1), channel_id=1, source_target_pairs={{0,6},{1,7},{2,0},{3,1},{4,2},{5,3},{6,4},{7,5},{8,14},{9,15},{10,... | collective-permute-start | bytes 294920 | tf_op jit(solution)/shard_map/ppermute | solution.py:30
  41.2 14.4 %collective-permute-start.2 = (bf16[12,8192]{1,0:T(8,128)(2,1)S(1)}, bf16[12,8192]{1,0:T(8,128)(2,1)S(1)}, u32[]{:S(2)}, u32[]{:S(2)}) collective-permute-start(bf16[12,8192]{1,0:T(8,128)(2,1)S(1)} %pad_maximum_fusion), channel_id=1, source_target_pairs={{0,4},{1,5},{2,6},{3,7},{4,0},{5,1},{6,2},{7,3},{8,12},{9,13},{10,... | collective-permute-start | bytes 589832 | tf_op jit(solution)/shard_map/ppermute | solution.py:30
  61.1 0.7 copy-start.1
Sparse Core Ops, SparseCore 0:
  9.8 33.5 all-gather.2
  73.2 30.1 reduce-scatter.1
